TPU v7x, 32 devices: a whole 2x2x4 slice. The times are simulated.
32 devices in a mesh: gx: 16 (over z, y, x), gy: 2 (over core).
Axes of the slice: x: 2, y: 2, z: 4, core: 2. Of those that a mesh axis runs over, the one named last changes fastest.
Arguments:
- forward_coeff: float32 [192, 4096], P(None, ('gx', 'gy')), may hold values from -6 to 6
- incident: float32 [192, 4096], P(None, ('gx', 'gy')), may hold values from -6 to 6
- cost_grad: float32 [192, 4096], P(None, ('gx', 'gy')), may hold values from -6 to 6
- tmat_real: float32 [4, 96, 96], replicated, may hold values from -0.21875 to 0.21875
- tmat_imag: float32 [4, 96, 96], replicated, may hold values from -0.21875 to 0.21875
- translation_real: float32 [10, 96, 96], replicated, may hold values from -0.125 to 0.125
- translation_imaginary: float32 [10, 96, 96], replicated, may hold values from -0.125 to 0.125
- neighbours: int32 [10, 4096], P(None, ('gx', 'gy')), may hold values from -1 to 4095, as said below
- particle_type: int32 [4096], P(('gx', 'gy')), may hold values from 0 to 3
Outputs:
- adjoint: float32 [192, 4096], P(None, ('gx', 'gy'))
- sensitivity: float32 [4, 192, 192], replicated
Inputs may be any that keep to these rules, and one draw needn't show every extreme that they name: `neighbours`: particles sit on a lattice cut into spatial tiles of 4 rows (wide direction) by 32 columns (short direction); tile t holds slots t * 128 to t * 128 + 127, tiles numbered along the short direction fastest, and slot p of a tile sits at row p // 32 and column p % 32 of its tile. An entry of -1 marks an empty slot. Any other entry names a particle whose lattice row and column differ from the particle's own by dr and dc with 0 < dr^2 + dc^2 <= 5; the entries of one particle's list name distinct particles.
All inputs are finite; a program needn't handle non-finite values.
Results may differ from a plain program's by a relative error of at most 0.0001.
Values sent between devices are 32-bit elements; how exact they have to be, the bound alone decides.
A program may use at most 64 MiB of HBM per device.

v0:
```python
import jax
import jax.numpy as jnp
from jax import lax
from jax.sharding import PartitionSpec as P

KRYLOV = 2


HIGH = lax.Precision.HIGHEST


def from_behind(block, axis, distance):
    devices = range(lax.axis_size(axis))
    route = [(i - distance, i) for i in devices if i - distance in devices]
    return lax.ppermute(block, axis, route)


def extended_2(x, sides, width):
    for axis, dim in sides:
        size, length = (lax.axis_size(axis), x.shape[dim])
        up = [(i, (i + 1) % size) for i in range(size - 1)]
        down = [(j, i) for i, j in up]
        last = lax.slice_in_dim(x, length - width, length, axis=dim)
        first = lax.slice_in_dim(x, 0, width, axis=dim)
        before = lax.ppermute(last, axis, up)
        after = lax.ppermute(first, axis, down)
        x = jnp.concatenate([before, x, after], axis=dim)
    return x


def complex_blocks(real_part, imag_part):
    upper_rows = jnp.concatenate([real_part, -imag_part], axis=2)
    lower_rows = jnp.concatenate([imag_part, real_part], axis=2)
    return jnp.concatenate([upper_rows, lower_rows], axis=1)


def small_solve(normal, right, steps):
    factor = jnp.linalg.cholesky(normal)
    forward_vals = []
    for row_index in range(steps):
        partial_sum = right[row_index]
        for col_index in range(row_index):
            partial_sum = partial_sum - factor[row_index, col_index] * forward_vals[col_index]
        forward_vals.append(partial_sum / factor[row_index, row_index])
    backward_vals = [None] * steps
    for row_index in reversed(range(steps)):
        partial_sum = forward_vals[row_index]
        for col_index in range(row_index + 1, steps):
            partial_sum = partial_sum - factor[col_index, row_index] * backward_vals[col_index]
        backward_vals[row_index] = partial_sum / factor[row_index, row_index]
    return backward_vals


def fold_wide(partial_value, dim):
    centre = jnp.take(partial_value, 1, axis=dim)
    for offset, piece in (
        (1, jnp.take(partial_value, 2, axis=dim)),
        (-1, jnp.take(partial_value, 0, axis=dim)),
    ):
        centre = centre + from_behind(piece, "gx", offset)
    return centre


def fold_short(partial_value, dim):
    centre = jnp.take(partial_value, 1, axis=dim)
    for offset, piece in (
        (1, jnp.take(partial_value, 2, axis=dim)),
        (-1, jnp.take(partial_value, 0, axis=dim)),
    ):
        centre = centre + from_behind(piece, "gy", offset)
    return centre


def body(
    forward_coeff,
    incident,
    cost_grad,
    tmat_real,
    tmat_imag,
    translation_real,
    translation_imaginary,
    neighbours,
    particle_type,
):
    width = forward_coeff.shape[0]
    local_count = forward_coeff.shape[1]
    kinds = tmat_real.shape[0]
    slots = translation_real.shape[0]
    steps = KRYLOV
    tmats = complex_blocks(tmat_real, tmat_imag)
    trans = complex_blocks(translation_real, translation_imaginary)
    tmat_stack = jnp.swapaxes(tmats, 1, 2).reshape(kinds * width, width)
    trans_adj = jnp.swapaxes(trans, 1, 2)
    kind_ids = jnp.arange(kinds, dtype=jnp.int32)
    type_mask = (particle_type[None, :] == kind_ids[:, None]).astype(jnp.float32)
    short_count = lax.axis_size("gy")
    tile = neighbours // local_count
    offset_x = tile // short_count - lax.axis_index("gx")
    offset_y = tile % short_count - lax.axis_index("gy")
    inner = neighbours % local_count
    target = (offset_x + 1) * (3 * local_count) + (offset_y + 1) * local_count + inner
    target = jnp.where(neighbours >= 0, target, 9 * local_count)
    flat_target = target.reshape(-1)
    extended = extended_2(
        forward_coeff.reshape(width, 1, 1, local_count), (("gx", 1), ("gy", 2)), 1
    )
    extended = jnp.concatenate(
        [extended.reshape(width, 9 * local_count), jnp.zeros((width, 1), jnp.float32)], axis=1
    )
    gathered = extended[:, target]
    exciting = incident + jnp.einsum("sdc,csp->dp", trans, gathered, precision=HIGH)
    beta = jnp.sqrt(lax.psum(jnp.sum(cost_grad * cost_grad), ("gx", "gy")))
    basis = [cost_grad / beta]
    columns = []
    for column in range(steps):
        vector = basis[column]
        all_kinds = jnp.dot(tmat_stack, vector, precision=HIGH).reshape(kinds, width, local_count)
        scaled = jnp.sum(type_mask[:, None, :] * all_kinds, axis=0)
        translated = jnp.einsum("sdc,cp->dsp", trans_adj, scaled, precision=HIGH).reshape(
            width, slots * local_count
        )
        collected = (
            jnp.zeros((width, 9 * local_count + 1), jnp.float32).at[:, flat_target].add(translated)
        )
        partial_value = collected[:, : 9 * local_count].reshape(width, 3, 3, local_count)
        summed = fold_short(fold_wide(partial_value, 1), 1)
        image = vector - summed
        local_dots = jnp.stack([jnp.sum(vec_item * image) for vec_item in basis])
        projections, squares = lax.psum((local_dots, jnp.sum(image * image)), ("gx", "gy"))
        for row_index in range(column + 1):
            image = image - projections[row_index] * basis[row_index]
        height = jnp.sqrt(squares - jnp.sum(projections * projections))
        columns.append(
            jnp.concatenate(
                [projections, height[None], jnp.zeros((steps - column - 1,), jnp.float32)]
            )
        )
        basis.append(image / height)
    hessen = jnp.stack(columns, axis=1)
    normal = jnp.dot(hessen.T, hessen, precision=HIGH)
    weights = small_solve(normal, beta * hessen[0], steps)
    adjoint = weights[0] * basis[0]
    column = 1
    adjoint = adjoint + weights[column] * basis[column]
    masked = adjoint[None, :, :] * type_mask[:, None, :]
    local_terms = jnp.einsum("kcp,dp->kcd", masked, exciting, precision=HIGH)
    sensitivity = lax.psum(local_terms, ("gx", "gy"))
    return (adjoint, sensitivity)


def solution(mesh):
    placed = (
        P(None, ("gx", "gy")),
        P(None, ("gx", "gy")),
        P(None, ("gx", "gy")),
        P(),
        P(),
        P(),
        P(),
        P(None, ("gx", "gy")),
        P(("gx", "gy")),
    )
    return jax.shard_map(
        body, mesh=mesh, in_specs=placed, out_specs=(P(None, ("gx", "gy")), P()), check_vma=False
    )
```

profile of v0, /device:TPU:13, one launch (start us, length us, event | category | flops | bytes accessed | tf_op | source)
XLA Modules:
  0.0 368.8 jit_solution(1161456165761627695)
XLA Ops:
  8.8 39.8 %psum.42 = f32[]{:T(128)} all-reduce(f32[]{:T(128)} %multiply_reduce_fusion.5), channel_id=1, replica_groups=mesh['gx'=16,'gy'=2] {'gx','gy'}, use_global_device_ids=true, to_apply=%region_1.2 | all-reduce | flops 1 | bytes 8 | tf_op jit(solution)/shard_map/psum | solution.py:112
  52.6 1.8 fusion.10
  54.5 1.7 fusion.4
  57.0 8.3 %scatter_custom_fusion = f32[192,1153]{0,1:T(8,128)S(1)} fusion(s32[1280]{0:T(1024)S(1)} %fusion.50, f32[1280,192]{1,0:T(8,128)S(1)} %bitcast.122, f32[]{:T(128)} %constant.178.clone.1), kind=kCustom, calls=%fused_computation.21 | custom fusion | flops 245760 | bytes 885508 | tf_op jit(solution)/shard_map/scatter-add | solution.py:123
  65.7 3.1 collective-permute-start
  69.0 3.1 collective-permute-start.1
  72.1 2.2 collective-permute-start.8
  74.3 4.0 %collective-permute-start.9 = (f32[192,1,1,128]{3,0,2,1:T(8,128)S(1)}, f32[192,1,1,128]{3,0,2,1:T(8,128)S(1)}, u32[]{:S(2)}, u32[]{:S(2)}) collective-permute-start(f32[192,1,1,128]{3,0,2,1:T(8,128)S(1)} %bitcast.125), channel_id=1, source_target_pairs={{2,0},{4,2},{6,4},{8,6},{10,8},{12,10},{14,12},{16,14},{18,16},{20... | collective-permute-start | bytes 294920 | tf_op jit(solution)/shard_map/ppermute | solution.py:26
  78.5 7.4 %collective-permute-done.1 = f32[192,3,128]{2,0,1:T(8,128)S(1)} collective-permute-done((f32[192,3,128]{2,0,1:T(8,128)S(1)}, f32[192,3,128]{2,0,1:T(8,128)S(1)}, u32[]{:S(2)}, u32[]{:S(2)}) %collective-permute-start.1) | collective-permute-done | bytes 294944 | tf_op jit(solution)/shard_map/ppermute | solution.py:15
  87.3 3.0 collective-permute-start.3
  92.5 4.4 %collective-permute-start.11 = (f32[192,3,1,128]{3,0,2,1:T(8,128)}, f32[192,3,1,128]{3,0,2,1:T(8,128)}, u32[]{:S(2)}, u32[]{:S(2)}) collective-permute-start(f32[192,3,1,128]{3,0,2,1:T(8,128)} %pad_maximum_fusion.1), channel_id=1, source_target_pairs={{1,0},{3,2},{5,4},{7,6},{9,8},{11,10},{13,12},{15,14},{17,16},{19,... | collective-permute-start | bytes 884744 | tf_op jit(solution)/shard_map/ppermute | solution.py:26
  97.7 36.8 %all-reduce.2 = (f32[]{:T(128)}, f32[1]{0:T(128)}) all-reduce(f32[]{:T(128)} %get-tuple-element.78, f32[1]{0:T(128)} %bitcast.14), channel_id=1, replica_groups=mesh['gx'=16,'gy'=2] {'gx','gy'}, use_global_device_ids=true, to_apply=%region_7.14 | all-reduce | flops 2 | bytes 16 | tf_op jit(solution)/shard_map/psum | solution.py:129
  136.9 1.8 fusion.11
  138.7 1.7 fusion.7
  140.9 8.4 %scatter_custom_fusion.1 = f32[192,1153]{0,1:T(8,128)S(1)} fusion(s32[1280]{0:T(1024)} %copy-done.15, f32[1280,192]{1,0:T(8,128)S(1)} %bitcast.123, f32[]{:T(128)} %constant.178.clone.1), kind=kCustom, calls=%fused_computation.19 | custom fusion | flops 245760 | bytes 886016 | tf_op jit(solution)/shard_map/scatter-add | solution.py:123
  150.4 3.4 collective-permute-start.4
  154.7 3.0 collective-permute-start.5
  159.5 4.1 %gather_fusion = f32[1280,192]{1,0:T(8,128)} fusion(f32[192,1153]{0,1:T(8,128)S(1)} %concatenate.43, s32[2048]{0:T(1024)S(1)} %pad_clamp_fusion), kind=kCustom, calls=%fused_computation | custom fusion | bytes 1971200 | tf_op jit(solution)/shard_map/gather | solution.py:110
  163.6 5.7 %fusion.13 = f32[192,128,1]{1,0,2:T(8,128)S(1)} fusion(f32[192,128]{1,0:T(8,128)S(1)} %copy-done.18, f32[192,10,128]{0,2,1:T(8,128)} %bitcast.121, f32[10,96,96]{1,2,0:T(8,128)S(1)} %copy-done.7, f32[10,96,96]{1,2,0:T(8,128)S(1)} %copy.23, f32[10,96,96]{1,2,0:T(8,128)S(1)} %copy-done.4), kind=kOutput, calls=%fused_computation.16 | convolution fusion | flops 567361536 | bytes 2285568 | tf_op jit(solution)/shard_map/sdc,csp->dp/dot_general | solution.py:111
  171.7 5.2 %collective-permute-start.7 = (f32[192,128]{1,0:T(8,128)S(1)}, f32[192,128]{1,0:T(8,128)S(1)}, u32[]{:S(2)}, u32[]{:S(2)}) collective-permute-start(f32[192,128]{1,0:T(8,128)S(1)} %get-tuple-element.93), channel_id=1, source_target_pairs={{1,0},{3,2},{5,4},{7,6},{9,8},{11,10},{13,12},{15,14},{17,16},{19,... | collective-permute-start | bytes 294920 | tf_op jit(solution)/shard_map/ppermute | solution.py:15
  180.0 39.4 %all-reduce.1 = (f32[]{:T(128)}, f32[2]{0:T(128)S(1)}) all-reduce(f32[]{:T(128)} %get-tuple-element.75, f32[2]{0:T(128)S(1)} %pad_maximum_fusion.3), channel_id=1, replica_groups=mesh['gx'=16,'gy'=2] {'gx','gy'}, use_global_device_ids=true, to_apply=%region_14.21 | all-reduce | flops 3 | bytes 24 | tf_op jit(solution)/shard_map/psum | solution.py:129
  229.5 1.7 fusion.18
  231.2 128.7 %all-reduce.5.cloned.1.call-done = f32[4,192,192]{2,1,0:T(8,128)} async-done(((f32[4,192,192]{2,1,0:T(8,128)}), f32[4,192,192]{2,1,0:T(8,128)}) %all-reduce.5.cloned.1.call-update) | async-done | bytes 589840 | tf_op jit(solution)/shard_map/psum | solution.py:147
  359.9 2.1 copy.46
  (102 shorter events, 24.2 us)
Async XLA Ops:
  7.2 45.2 %copy-start.1 = (f32[10,96,96]{2,1,0:T(8,128)S(1)}, f32[10,96,96]{2,1,0:T(8,128)}, u32[]{:S(2)}) copy-start(f32[10,96,96]{2,1,0:T(8,128)} %param.26) | copy-start | bytes 1105924
  7.2 352.7 %all-reduce.5.cloned.1.call-start = ((), (), s32[]{:S(2)}) async-start(), calls=%async_computation | async-start | bytes 1572864 | tf_op jit(solution)/shard_map/psum | solution.py:147
  57.0 8.4 %copy-start.15 = (s32[1280]{0:T(1024)}, s32[1280]{0:T(1024)S(1)}, u32[]{:S(2)}) copy-start(s32[1280]{0:T(1024)S(1)} %fusion.50) | copy-start | bytes 15364
  65.4 6.7 %copy-start.8 = (f32[192,128]{1,0:T(8,128)S(1)}, f32[192,128]{1,0:T(8,128)}, u32[]{:S(2)}) copy-start(f32[192,128]{1,0:T(8,128)} %param.21) | copy-start | bytes 294916
  65.7 12.8 %collective-permute-start = (f32[192,3,128]{2,0,1:T(8,128)S(1)}, f32[192,3,128]{2,0,1:T(8,128)S(1)}, u32[]{:S(2)}, u32[]{:S(2)}) collective-permute-start(f32[192,3,128]{2,0,1:T(8,128)S(1)} %bitcast.128), channel_id=1, source_target_pairs={{0,2},{2,4},{4,6},{6,8},{8,10},{10,12},{12,14},{14,16},{16,18},{18... | collective-permute-start | bytes 884744 | tf_op jit(solution)/shard_map/ppermute | solution.py:15
  69.0 17.0 %collective-permute-start.1 = (f32[192,3,128]{2,0,1:T(8,128)S(1)}, f32[192,3,128]{2,0,1:T(8,128)S(1)}, u32[]{:S(2)}, u32[]{:S(2)}) collective-permute-start(f32[192,3,128]{2,0,1:T(8,128)S(1)} %bitcast.129), channel_id=1, source_target_pairs={{2,0},{4,2},{6,4},{8,6},{10,8},{12,10},{14,12},{16,14},{18,16},{20... | collective-permute-start | bytes 884744 | tf_op jit(solution)/shard_map/ppermute | solution.py:15
  72.1 18.3 %collective-permute-start.8 = (f32[192,1,1,128]{3,0,2,1:T(8,128)S(1)}, f32[192,1,1,128]{3,0,2,1:T(8,128)S(1)}, u32[]{:S(2)}, u32[]{:S(2)}) collective-permute-start(f32[192,1,1,128]{3,0,2,1:T(8,128)S(1)} %bitcast.124), channel_id=1, source_target_pairs={{0,2},{2,4},{4,6},{6,8},{8,10},{10,12},{12,14},{14,16},{16,18},{18... | collective-permute-start | bytes 294920 | tf_op jit(solution)/shard_map/ppermute | solution.py:25
  74.3 16.1 %collective-permute-start.9 = (f32[192,1,1,128]{3,0,2,1:T(8,128)S(1)}, f32[192,1,1,128]{3,0,2,1:T(8,128)S(1)}, u32[]{:S(2)}, u32[]{:S(2)}) collective-permute-start(f32[192,1,1,128]{3,0,2,1:T(8,128)S(1)} %bitcast.125), channel_id=1, source_target_pairs={{2,0},{4,2},{6,4},{8,6},{10,8},{12,10},{14,12},{16,14},{18,16},{20... | collective-permute-start | bytes 294920 | tf_op jit(solution)/shard_map/ppermute | solution.py:26
  78.5 58.4 %copy-start.11 = (f32[4,96,96]{2,1,0:T(8,128)S(1)}, f32[4,96,96]{2,1,0:T(8,128)}, u32[]{:S(2)}) copy-start(f32[4,96,96]{2,1,0:T(8,128)} %param.25) | copy-start | bytes 442372
  78.5 58.4 %copy-start.13 = (f32[4,96,96]{2,1,0:T(8,128)S(1)}, f32[4,96,96]{2,1,0:T(8,128)}, u32[]{:S(2)}) copy-start(f32[4,96,96]{2,1,0:T(8,128)} %copy-done.12) | copy-start | bytes 442372
  78.5 58.4 %copy-start.17 = (f32[4,96,96]{2,1,0:T(8,128)S(1)}, f32[4,96,96]{2,1,0:T(8,128)}, u32[]{:S(2)}) copy-start(f32[4,96,96]{2,1,0:T(8,128)} %param.24) | copy-start | bytes 442372
  86.0 11.0 %collective-permute-start.2 = (f32[192,128]{1,0:T(8,128)S(1)}, f32[192,128]{1,0:T(8,128)S(1)}, u32[]{:S(2)}, u32[]{:S(2)}) collective-permute-start(f32[192,128]{1,0:T(8,128)S(1)} %get-tuple-element.94), channel_id=1, source_target_pairs={{0,1},{2,3},{4,5},{6,7},{8,9},{10,11},{12,13},{14,15},{16,17},{18,... | collective-permute-start | bytes 294920 | tf_op jit(solution)/shard_map/ppermute | solution.py:15
  87.3 9.7 %collective-permute-start.3 = (f32[192,128]{1,0:T(8,128)S(1)}, f32[192,128]{1,0:T(8,128)S(1)}, u32[]{:S(2)}, u32[]{:S(2)}) collective-permute-start(f32[192,128]{1,0:T(8,128)S(1)} %get-tuple-element.95), channel_id=1, source_target_pairs={{1,0},{3,2},{5,4},{7,6},{9,8},{11,10},{13,12},{15,14},{17,16},{19,... | collective-permute-start | bytes 294920 | tf_op jit(solution)/shard_map/ppermute | solution.py:15
  91.1 47.6 %copy-start.3 = (f32[10,96,96]{1,2,0:T(8,128)S(1)}, f32[10,96,96]{1,2,0:T(8,128)}, u32[]{:S(2)}) copy-start(f32[10,96,96]{1,2,0:T(8,128)} %copy-done.2) | copy-start | bytes 1105924
  91.1 47.6 %copy-start.6 = (f32[10,96,96]{1,2,0:T(8,128)S(1)}, f32[10,96,96]{1,2,0:T(8,128)}, u32[]{:S(2)}) copy-start(f32[10,96,96]{1,2,0:T(8,128)} %copy-done.5) | copy-start | bytes 1105924
  91.1 66.6 %collective-permute-start.10 = (f32[192,3,1,128]{3,0,2,1:T(8,128)}, f32[192,3,1,128]{3,0,2,1:T(8,128)}, u32[]{:S(2)}, u32[]{:S(2)}) collective-permute-start(f32[192,3,1,128]{3,0,2,1:T(8,128)} %pad_maximum_fusion.1), channel_id=1, source_target_pairs={{0,1},{2,3},{4,5},{6,7},{8,9},{10,11},{12,13},{14,15},{16,17},{18,... | collective-permute-start | bytes 884744 | tf_op jit(solution)/shard_map/ppermute | solution.py:25
  92.5 65.2 %collective-permute-start.11 = (f32[192,3,1,128]{3,0,2,1:T(8,128)}, f32[192,3,1,128]{3,0,2,1:T(8,128)}, u32[]{:S(2)}, u32[]{:S(2)}) collective-permute-start(f32[192,3,1,128]{3,0,2,1:T(8,128)} %pad_maximum_fusion.1), channel_id=1, source_target_pairs={{1,0},{3,2},{5,4},{7,6},{9,8},{11,10},{13,12},{15,14},{17,16},{19,... | collective-permute-start | bytes 884744 | tf_op jit(solution)/shard_map/ppermute | solution.py:26
  150.4 18.9 %collective-permute-start.4 = (f32[192,3,128]{2,0,1:T(8,128)}, f32[192,3,128]{2,0,1:T(8,128)}, u32[]{:S(2)}, u32[]{:S(2)}) collective-permute-start(f32[192,3,128]{2,0,1:T(8,128)} %bitcast.26), channel_id=1, source_target_pairs={{0,2},{2,4},{4,6},{6,8},{8,10},{10,12},{12,14},{14,16},{16,18},{18... | collective-permute-start | bytes 884744 | tf_op jit(solution)/shard_map/ppermute | solution.py:15
  154.7 14.7 %collective-permute-start.5 = (f32[192,3,128]{2,0,1:T(8,128)}, f32[192,3,128]{2,0,1:T(8,128)}, u32[]{:S(2)}, u32[]{:S(2)}) collective-permute-start(f32[192,3,128]{2,0,1:T(8,128)} %bitcast.27), channel_id=1, source_target_pairs={{2,0},{4,2},{6,4},{8,6},{10,8},{12,10},{14,12},{16,14},{18,16},{20... | collective-permute-start | bytes 884744 | tf_op jit(solution)/shard_map/ppermute | solution.py:15
  159.4 4.1 %copy-start.4 = (f32[10,96,96]{1,2,0:T(8,128)S(1)}, f32[10,96,96]{1,2,0:T(8,128)}, u32[]{:S(2)}) copy-start(f32[10,96,96]{1,2,0:T(8,128)} %copy-done.2) | copy-start | bytes 1105924
  159.4 4.1 %copy-start.7 = (f32[10,96,96]{1,2,0:T(8,128)S(1)}, f32[10,96,96]{1,2,0:T(8,128)}, u32[]{:S(2)}) copy-start(f32[10,96,96]{1,2,0:T(8,128)} %copy-done.5) | copy-start | bytes 1105924
  170.4 7.1 %collective-permute-start.6 = (f32[192,128]{1,0:T(8,128)S(1)}, f32[192,128]{1,0:T(8,128)S(1)}, u32[]{:S(2)}, u32[]{:S(2)}) collective-permute-start(f32[192,128]{1,0:T(8,128)S(1)} %get-tuple-element.92), channel_id=1, source_target_pairs={{0,1},{2,3},{4,5},{6,7},{8,9},{10,11},{12,13},{14,15},{16,17},{18,... | collective-permute-start | bytes 294920 | tf_op jit(solution)/shard_map/ppermute | solution.py:15
  171.7 6.1 %collective-permute-start.7 = (f32[192,128]{1,0:T(8,128)S(1)}, f32[192,128]{1,0:T(8,128)S(1)}, u32[]{:S(2)}, u32[]{:S(2)}) collective-permute-start(f32[192,128]{1,0:T(8,128)S(1)} %get-tuple-element.93), channel_id=1, source_target_pairs={{1,0},{3,2},{5,4},{7,6},{9,8},{11,10},{13,12},{15,14},{17,16},{19,... | collective-permute-start | bytes 294920 | tf_op jit(solution)/shard_map/ppermute | solution.py:15
  229.5 132.5 %copy-start.9 = (f32[192,128]{1,0:T(8,128)}, f32[192,128]{1,0:T(8,128)S(1)}, u32[]{:S(2)}) copy-start(f32[192,128]{1,0:T(8,128)S(1)} %multiply_add_fusion) | copy-start | bytes 294916
  (8 other events, 15.4 us)
Sparse Core Ops, SparseCore 0:
  231.3 128.5 all-reduce.4
where the time goes:
time: 374 us; the launch traced here: 369 us
  waiting for transfers between devices  136 us (36%)
  blocking collectives  116 us (31%)
  starting transfers between devices  35.4 us (9%)
  other arithmetic  29.2 us (8%)
  between operations  23.7 us (6%)
  matrix products  14.7 us (4%)
  local copies, waits for them, and re-layouts  13.3 us (4%)
    psum x1, waiting for transfers between devices, body(): sensitivity = lax.psum(local_terms, ('gx', 'gy'))  129 us
    psum x2, blocking collectives, body(): lax.psum((local_dots, jnp.sum(image * image)), ('gx', 'gy'))  76.2 us
    psum x1, blocking collectives, body(): beta = jnp.sqrt(lax.psum(jnp.sum(cost_grad * cost_grad), ('gx', 'gy')))  39.8 us
    ppermute x8, starting transfers between devices, from_behind(): return lax.ppermute(block, axis, route)  23.3 us
    scatter-add x2, other arithmetic, body(): jnp.zeros((width, 9 * local_count + 1), jnp.float32).at[:, flat_target]  16.7 us
    ppermute x2, starting transfers between devices, extended_2(): after = lax.ppermute(first, axis, down)  8.43 us
    ppermute x8, waiting for transfers between devices, from_behind(): return lax.ppermute(block, axis, route)  7.76 us
  transfers between devices with their start and end apart: 13, of which 3 were waited for; matrix products, arithmetic and copies ran while one was open for 8% of the time, Pallas kernels for 0%

commit v1 on v0

v1 whole, which is shorter than its diff:
```python
import functools

import jax
import jax.numpy as jnp
from jax import lax
from jax.experimental import pallas as pl
from jax.experimental.pallas import tpu as pltpu
from jax.sharding import PartitionSpec as P

MESH = pl.DeviceIdType.MESH
COLS = 32
REACH = 2
F32 = jnp.float32
BF16 = jnp.bfloat16


def split(x):
    hi = x.astype(BF16)
    return hi, (x - hi.astype(F32)).astype(BF16)


def dot(a, b, rhs_dim=0):
    return lax.dot_general(a, b, (((1,), (rhs_dim,)), ((), ())), preferred_element_type=F32)


def dot3(a, b, rhs_dim=0):
    return dot(a[0], b[0], rhs_dim) + (dot(a[1], b[0], rhs_dim) + dot(a[0], b[1], rhs_dim))


def kernel(
    n_gx, n_gy, chunk,
    f_ref, inc_ref, g_ref, tr_ref, ti_ref, xr_ref, xi_ref, nbr_ref, kind_ref,
    adj_ref, sens_ref,
    t_hi, t_lo, w_hi, w_lo, one_ref, two_ref, y_hi, y_lo, fext, pack, coll, part, work,
    s_all, s_recv, s_mine, s_out, gram, gram_recv,
    f_send, f_recv, p_send, p_recv, gram_sem, rs_send, rs_recv, ag_sem,
):
    width, count = f_ref.shape
    half = width // 2
    kinds, slots = tr_ref.shape[0], xr_ref.shape[0]
    rows = count // COLS
    devices = n_gx * n_gy
    owners = kinds * width // chunk
    gx, gy = lax.axis_index("gx"), lax.axis_index("gy")
    me = gx * n_gy + gy

    def each_peer(body):
        def step(j, carry):
            peer = lax.rem(me + 1 + j, devices)
            body(j, peer, (peer // n_gy, lax.rem(peer, n_gy)))
            return carry
        lax.fori_loop(0, devices - 1, step, 0)

    barrier = pltpu.get_barrier_semaphore()
    each_peer(lambda j, peer, place: pl.semaphore_signal(
        barrier, inc=1, device_id=place, device_id_type=MESH))

    edge, side = REACH * COLS, REACH * rows
    above, below = (lax.rem(gx + n_gx - 1, n_gx), lax.rem(gx + 1, n_gx))
    left, right = (lax.rem(gy + n_gy - 1, n_gy), lax.rem(gy + 1, n_gy))
    blocks = (
        (0, edge, (above, gy), (below, gy)),
        (edge, edge, (below, gy), (above, gy)),
        (2 * edge, side, (gx, left), (gx, right)),
        (2 * edge + side, side, (gx, right), (gx, left)),
        (2 * edge + 2 * side, 8, (above, left), (below, right)),
        (2 * edge + 2 * side + 8, 8, (above, right), (below, left)),
        (2 * edge + 2 * side + 16, 8, (below, left), (above, right)),
        (2 * edge + 2 * side + 24, 8, (below, right), (above, left)),
    )
    small = 2 * edge
    last = COLS - REACH
    far = rows - REACH
    pieces = (
        (blocks[2][0], 0, rows, last),
        (blocks[3][0], 0, rows, 0),
        (blocks[4][0], far, REACH, last),
        (blocks[5][0], far, REACH, 0),
        (blocks[6][0], 0, REACH, last),
        (blocks[7][0], 0, REACH, 0),
    )

    fext[pl.ds(0, count), :] = f_ref[...].T
    pack[...] = jnp.zeros_like(pack)
    for start, row, number, column in pieces:
        for r in range(number):
            pack[pl.ds(start - small + REACH * r, REACH), :] = fext[
                pl.ds((row + r) * COLS + column, REACH), :]

    nbr = nbr_ref[...]
    tile, inner = nbr // count, nbr % count
    off_x, off_y = tile // n_gy - gx, tile % n_gy - gy
    row, col = inner // COLS, inner % COLS
    at_edge = jnp.where(off_x < 0, inner - (count - edge), inner + edge)
    at_side = 2 * edge + jnp.where(off_y < 0, 0, side) + row * REACH + jnp.where(off_y < 0, col - last, col)
    at_corner = (
        2 * edge + 2 * side + jnp.where(off_x < 0, 0, 16) + jnp.where(off_y < 0, 0, 8)
        + jnp.where(off_x < 0, row - far, row) * REACH + jnp.where(off_y < 0, col - last, col)
    )
    outside = jnp.where(off_y == 0, at_edge, jnp.where(off_x == 0, at_side, at_corner))
    target = jnp.where((off_x == 0) & (off_y == 0), inner, count + outside)
    target = jnp.where(nbr >= 0, target, -1)
    kind_row = kind_ref[...]
    pad = 16 - slots - 1
    meta = jnp.concatenate([target, kind_row] + ([jnp.zeros((pad, count), jnp.int32)] if pad else []), axis=0)
    meta_t = meta.astype(F32).T.astype(jnp.int32)
    extent = fext.shape[0]
    for s in range(slots):
        down = lax.broadcasted_iota(jnp.int32, (extent, count), 0)
        one_ref[:, pl.ds(s * count, count)] = jnp.where(down == target[s:s + 1, :], 1.0, 0.0).astype(BF16)
        across = lax.broadcasted_iota(jnp.int32, (count, extent), 1)
        two_ref[pl.ds(s * count, count), :] = jnp.where(across == meta_t[:, s:s + 1], 1.0, 0.0).astype(BF16)
    kind_col = meta_t[:, slots:slots + 1]

    def prepare(real_ref, imag_ref, hi_ref, lo_ref, number):
        for k in range(number):
            real, imag = real_ref[k], imag_ref[k]
            for start, block in (
                (0, jnp.concatenate([real, -imag], axis=1)),
                (half, jnp.concatenate([imag, real], axis=1)),
            ):
                hi, lo = split(block)
                hi_ref[k, pl.ds(start, half), :] = hi
                lo_ref[k, pl.ds(start, half), :] = lo

    prepare(tr_ref, ti_ref, t_hi, t_lo, kinds)
    prepare(xr_ref, xi_ref, w_hi, w_lo, slots)

    pl.semaphore_wait(barrier, devices - 1)

    f_copies = []
    for b, (start, size, _, place) in enumerate(blocks):
        if b == 0:
            src = fext.at[pl.ds(count - edge, edge)]
        elif b == 1:
            src = fext.at[pl.ds(0, edge)]
        else:
            src = pack.at[pl.ds(start - small, size)]
        copy = pltpu.make_async_remote_copy(
            src_ref=src, dst_ref=fext.at[pl.ds(count + start, size)],
            send_sem=f_send.at[b], recv_sem=f_recv.at[b], device_id=place, device_id_type=MESH)
        copy.start()
        f_copies.append(copy)

    def push(index, x):
        hi, lo = split(x)
        scaled = jnp.zeros((count, width), F32)
        for k in range(kinds):
            mask = jnp.where(kind_col == k, 1.0, 0.0).astype(BF16)
            scaled = scaled + dot3((hi * mask, lo * mask), (t_hi[k], t_lo[k]))
        pair = split(scaled)
        for s in range(slots):
            h, l = split(dot3(pair, (w_hi[s], w_lo[s])))
            y_hi[pl.ds(s * count, count), :] = h
            y_lo[pl.ds(s * count, count), :] = l
        coll[index] = dot(one_ref[...], y_hi[...]) + dot(one_ref[...], y_lo[...])
        copies = []
        for b, (start, size, place, _) in enumerate(blocks):
            copy = pltpu.make_async_remote_copy(
                src_ref=coll.at[index, pl.ds(count + start, size)], dst_ref=part.at[index, pl.ds(start, size)],
                send_sem=p_send.at[index, b], recv_sem=p_recv.at[index, b], device_id=place, device_id_type=MESH)
            copy.start()
            copies.append(copy)
        return copies

    def pull(index, copies):
        for copy in copies:
            copy.wait_recv()
        work[...] = coll[index, pl.ds(0, count), :]
        work[pl.ds(count - edge, edge), :] += part[index, pl.ds(0, edge), :]
        work[pl.ds(0, edge), :] += part[index, pl.ds(edge, edge), :]
        for start, row, number, column in pieces:
            for r in range(number):
                where = pl.ds((row + r) * COLS + column, REACH)
                work[where, :] += part[index, pl.ds(start + REACH * r, REACH), :]
        return work[...]

    def scatter_terms(index, field, exciting):
        hi, lo = split(field)
        for k in range(kinds):
            mask = jnp.where(kind_row == k, 1.0, 0.0).astype(BF16)
            s_all[index, pl.ds(k * width, width), :] = dot3((hi * mask, lo * mask), exciting)

        def send(j, peer, place):
            def go():
                pltpu.make_async_remote_copy(
                    src_ref=s_all.at[index, pl.ds(pl.multiple_of(peer * chunk, 8), chunk)],
                    dst_ref=s_recv.at[index, devices - 2 - j],
                    send_sem=rs_send.at[index], recv_sem=rs_recv.at[index],
                    device_id=place, device_id_type=MESH).start()
            if owners == devices:
                go()
            else:
                pl.when(peer < owners)(go)
        each_peer(send)

    def wait_bytes(sem, ref):
        pltpu.make_async_copy(ref, ref, sem).wait()

    g_t = g_ref[...].T
    first = push(0, g_t)

    for copy in f_copies:
        copy.wait_recv()
    ext = split(fext[...])
    exciting_t = inc_ref[...].T
    for s in range(slots):
        pick = two_ref[pl.ds(s * count, count), :]
        pair = (dot(pick, ext[0]).astype(BF16), dot(pick, ext[1]).astype(BF16))
        exciting_t = exciting_t + dot3(pair, (w_hi[s], w_lo[s]), 1)
    exciting = split(exciting_t)
    scatter_terms(0, g_ref[...], exciting)

    q0_t = pull(0, first)
    second = push(1, q0_t)
    q0 = q0_t.T
    scatter_terms(1, q0, exciting)
    q1_t = pull(1, second)

    for i, (a, b) in enumerate(
        ((g_t, g_t), (g_t, q0_t), (q0_t, q0_t), (g_t, q1_t), (q0_t, q1_t), (q1_t, q1_t))
    ):
        gram[i:i + 1, :] = jnp.sum(a * b, axis=0, keepdims=True)
    gram[6:8, :] = jnp.zeros((2, width), F32)
    each_peer(lambda j, peer, place: pltpu.make_async_remote_copy(
        src_ref=gram, dst_ref=gram_recv.at[devices - 2 - j],
        send_sem=gram_sem.at[0], recv_sem=gram_sem.at[1], device_id=place, device_id_type=MESH).start())
    wait_bytes(gram_sem.at[1], gram_recv)
    sums = jnp.sum(gram[...] + jnp.sum(gram_recv[...], axis=0), axis=1, keepdims=True)
    gg, gq, qq, gv, qv, vv = (sums[i:i + 1, :] for i in range(6))

    beta = jnp.sqrt(gg)
    c = gq / gg
    p2 = qq - c * gq
    p1 = jnp.sqrt(p2)
    gz = gv - c * gq
    pz = (qv - c * qq) - c * gz
    zz = vv - 2.0 * c * qv + c * c * qq
    h00, h10 = 1.0 - c, p1 / beta
    h01, h11 = gz / (beta * p1), 1.0 - pz / p2
    along = pz / p2
    h21 = jnp.sqrt(jnp.maximum(zz / p2 - h01 * h01 - along * along, 0.0))
    n00 = h00 * h00 + h10 * h10
    n01 = h00 * h01 + h10 * h11
    n11 = h01 * h01 + h11 * h11 + h21 * h21
    r0, r1 = beta * h00, beta * h01
    l00 = jnp.sqrt(n00)
    l10 = n01 / l00
    l11 = jnp.sqrt(n11 - l10 * l10)
    v0 = r0 / l00
    v1 = (r1 - l10 * v0) / l11
    w1 = v1 / l11
    w0 = (v0 - l10 * w1) / l00
    from_g, from_q = w0 / beta + w1 * c / p1, -w1 / p1
    adj_ref[...] = from_g * g_ref[...] + from_q * q0

    def reduce_mine():
        total = []
        for index in range(2):
            wait_bytes(rs_recv.at[index], s_recv.at[index])
            own = s_all[index, pl.ds(pl.multiple_of(me * chunk, 8), chunk), :]
            total.append(own + jnp.sum(s_recv[index], axis=0))
        mine = from_g * total[0] + from_q * total[1]
        s_mine[...] = mine
        each_peer(lambda j, peer, place: pltpu.make_async_remote_copy(
            src_ref=s_mine, dst_ref=s_out.at[pl.ds(pl.multiple_of(me * chunk, 8), chunk)],
            send_sem=ag_sem.at[0], recv_sem=ag_sem.at[1], device_id=place, device_id_type=MESH).start())
        s_out[pl.ds(pl.multiple_of(me * chunk, 8), chunk), :] = mine
        if owners > 1:
            wait_bytes(ag_sem.at[1], s_out.at[pl.ds(0, (owners - 1) * chunk)])
            for index in range(2):
                wait_bytes(rs_send.at[index], s_all.at[index, pl.ds(0, (owners - 1) * chunk)])
        wait_bytes(ag_sem.at[0], s_recv.at[0])

    if owners == devices:
        reduce_mine()
    else:
        pl.when(me < owners)(reduce_mine)

        @pl.when(me >= owners)
        def _():
            wait_bytes(ag_sem.at[1], s_out)
            for index in range(2):
                wait_bytes(rs_send.at[index], s_all.at[index])

    sens_ref[...] = s_out[...]
    for copy in f_copies + first + second:
        copy.wait_send()
    wait_bytes(gram_sem.at[0], gram_recv)


def body(n_gx, n_gy, forward_coeff, incident, cost_grad, tmat_real, tmat_imag, translation_real,
         translation_imaginary, neighbours, particle_type):
    width, count = forward_coeff.shape
    kinds, slots = tmat_real.shape[0], translation_real.shape[0]
    devices = n_gx * n_gy
    rows = count // COLS
    halo = 2 * REACH * COLS + 2 * REACH * rows + 32
    extent = count + halo
    total = kinds * width
    chunk = 8
    while total % chunk or total // chunk > devices:
        chunk += 8
    vmem = [pl.BlockSpec(memory_space=pltpu.VMEM)]
    adjoint, sensitivity = pl.pallas_call(
        functools.partial(kernel, n_gx, n_gy, chunk),
        out_shape=(
            jax.ShapeDtypeStruct((width, count), F32),
            jax.ShapeDtypeStruct((total, width), F32),
        ),
        in_specs=vmem * 9,
        out_specs=(vmem[0], vmem[0]),
        scratch_shapes=[
            pltpu.VMEM((kinds, width, width), BF16),
            pltpu.VMEM((kinds, width, width), BF16),
            pltpu.VMEM((slots, width, width), BF16),
            pltpu.VMEM((slots, width, width), BF16),
            pltpu.VMEM((extent, slots * count), BF16),
            pltpu.VMEM((slots * count, extent), BF16),
            pltpu.VMEM((slots * count, width), BF16),
            pltpu.VMEM((slots * count, width), BF16),
            pltpu.VMEM((extent, width), F32),
            pltpu.VMEM((2 * REACH * rows + 32, width), F32),
            pltpu.VMEM((2, extent, width), F32),
            pltpu.VMEM((2, halo, width), F32),
            pltpu.VMEM((count, width), F32),
            pltpu.VMEM((2, total, width), F32),
            pltpu.VMEM((2, devices - 1, chunk, width), F32),
            pltpu.VMEM((chunk, width), F32),
            pltpu.VMEM((total, width), F32),
            pltpu.VMEM((8, width), F32),
            pltpu.VMEM((devices - 1, 8, width), F32),
            pltpu.SemaphoreType.DMA((8,)),
            pltpu.SemaphoreType.DMA((8,)),
            pltpu.SemaphoreType.DMA((2, 8)),
            pltpu.SemaphoreType.DMA((2, 8)),
            pltpu.SemaphoreType.DMA((2,)),
            pltpu.SemaphoreType.DMA((2,)),
            pltpu.SemaphoreType.DMA((2,)),
            pltpu.SemaphoreType.DMA((2,)),
        ],
        compiler_params=pltpu.CompilerParams(
            collective_id=0, has_side_effects=True, vmem_limit_bytes=48 * 1024 * 1024),
    )(forward_coeff, incident, cost_grad, tmat_real, tmat_imag, translation_real,
      translation_imaginary, neighbours, particle_type.reshape(1, count))
    return adjoint, sensitivity.reshape(kinds, width, width)


def solution(mesh):
    spread = P(None, ("gx", "gy"))
    placed = (spread, spread, spread, P(), P(), P(), P(), spread, P(("gx", "gy")))
    return jax.shard_map(
        functools.partial(body, mesh.shape["gx"], mesh.shape["gy"]),
        mesh=mesh, in_specs=placed, out_specs=(spread, P()), check_vma=False)
```

time: 374 us -> 86.5 us (0.23); the launches traced: 369 us -> 85.2 us
  waiting for transfers between devices: 136 us -> 0 us
  blocking collectives: 116 us -> 0 us
  Pallas kernels: 0 us -> 75.1 us
  starting transfers between devices: 35.4 us -> 0 us
  other arithmetic: 29.2 us -> 0 us
  between operations: 23.7 us -> 0.66 us
  matrix products: 14.7 us -> 0 us
  local copies, waits for them, and re-layouts: 13.3 us -> 9.45 us
    psum x1 -> x0, waiting for transfers between devices: 129 us -> none  [body(): sensitivity = lax.psum(local_terms, ('gx', 'gy'))]
    psum x3 -> x0, blocking collectives: 116 us -> none  [the longest x2 76.2 us: body(): lax.psum((local_dots, jnp.sum(image * image)), ('gx', 'gy'))]
    pallas_call x0 -> x1, Pallas kernels: none -> 75.1 us  [body(): pl.pallas_call(functools.partial(kernel, n_gx, n_gy, chunk), out_shape=(j...]
    ppermute x12 -> x0, starting transfers between devices: 35.4 us -> none  [the longest x8 23.3 us: from_behind(): return lax.ppermute(block, axis, route)]
    scatter-add x2 -> x0, other arithmetic: 16.7 us -> none  [body(): jnp.zeros((width, 9 * local_count + 1), jnp.float32).at[:, flat_target]]
    dot_general x7 -> x0, matrix products: 14.7 us -> none  [the longest x1 5.71 us: body(): jnp.einsum('sdc,csp->dp', trans, gathered, precision=HIGH)]
    ppermute x12 -> x0, waiting for transfers between devices: 7.77 us -> none  [the longest x8 7.76 us: from_behind(): return lax.ppermute(block, axis, route)]
    gather x3 -> x0, local copies, waits for them, and re-layouts: 4.14 us -> none  [the longest x1 4.11 us: body(): gathered = extended[:, target]]
  transfers between devices with their start and end apart: 13 -> 0, of which waited for: 3 -> 0; matrix products, arithmetic and copies ran while one was open for 8% -> 0% of each run, Pallas kernels for 0% -> 0%
where the time goes in v1:
time: 86.5 us; the launch traced here: 85.2 us
  Pallas kernels  75.1 us (87%)
  local copies, waits for them, and re-layouts  9.45 us (11%)
    pallas_call x1, Pallas kernels, body(): pl.pallas_call(functools.partial(kernel, n_gx, n_gy, chunk), out_shape=(j...  75.1 us
    unnamed x20, local copies, waits for them, and re-layouts  9.45 us

profile of v1, /device:TPU:13, one launch (start us, length us, event | category | flops | bytes accessed | tf_op | source)
XLA Modules:
  0.0 85.2 jit_solution(12457814230605663147)
XLA Ops:
  0.6 0.0 copy-start.8
  0.6 0.6 copy-done.8
  1.3 0.0 copy-start
  1.3 1.0 %copy-done = f32[10,96,96]{2,1,0:T(8,128)S(1)} copy-done((f32[10,96,96]{2,1,0:T(8,128)S(1)}, f32[10,96,96]{2,1,0:T(8,128)}, u32[]{:S(2)}) %copy-start) | copy-done | bytes 368664
  2.3 0.0 copy-start.1
  2.3 1.0 %copy-done.1 = f32[10,96,96]{2,1,0:T(8,128)S(1)} copy-done((f32[10,96,96]{2,1,0:T(8,128)S(1)}, f32[10,96,96]{2,1,0:T(8,128)}, u32[]{:S(2)}) %copy-start.1) | copy-done | bytes 368664
  3.4 0.0 copy-start.2
  3.4 0.9 %copy-done.2 = f32[4,96,96]{2,1,0:T(8,128)S(1)} copy-done((f32[4,96,96]{2,1,0:T(8,128)S(1)}, f32[4,96,96]{2,1,0:T(8,128)}, u32[]{:S(2)}) %copy-start.2) | copy-done | bytes 147480
  4.3 0.0 copy-start.3
  4.3 0.9 %copy-done.3 = f32[4,96,96]{2,1,0:T(8,128)S(1)} copy-done((f32[4,96,96]{2,1,0:T(8,128)S(1)}, f32[4,96,96]{2,1,0:T(8,128)}, u32[]{:S(2)}) %copy-start.3) | copy-done | bytes 147480
  5.2 0.0 copy-start.4
  5.2 0.9 %copy-done.4 = f32[192,128]{1,0:T(8,128)S(1)} copy-done((f32[192,128]{1,0:T(8,128)S(1)}, f32[192,128]{1,0:T(8,128)}, u32[]{:S(2)}) %copy-start.4) | copy-done | bytes 98328
  6.1 0.0 copy-start.5
  6.1 0.9 %copy-done.5 = f32[192,128]{1,0:T(8,128)S(1)} copy-done((f32[192,128]{1,0:T(8,128)S(1)}, f32[192,128]{1,0:T(8,128)}, u32[]{:S(2)}) %copy-start.5) | copy-done | bytes 98328
  7.0 0.0 copy-start.6
  7.0 0.9 %copy-done.6 = f32[192,128]{1,0:T(8,128)S(1)} copy-done((f32[192,128]{1,0:T(8,128)S(1)}, f32[192,128]{1,0:T(8,128)}, u32[]{:S(2)}) %copy-start.6) | copy-done | bytes 98328
  7.9 0.0 copy-start.7
  7.9 0.7 copy-done.7
  8.6 75.1 %shard_map.104 = (f32[192,128]{1,0:T(8,128)S(1)}, f32[768,192]{1,0:T(8,128)S(1)}) custom-call(f32[192,128]{1,0:T(8,128)S(1)} %copy-done.4, f32[192,128]{1,0:T(8,128)S(1)} %copy-done.5, f32[192,128]{1,0:T(8,128)S(1)} %copy-done.6, f32[4,96,96]{2,1,0:T(8,128)S(1)} %copy-done.2, f32[4,96,96]{2,1,0:T(8,128)S(1)} %copy-done.3, f32[10,96,96]{2,1,0:T(8,128)S(1)} %copy-done, ...), custom_call_target="tpu_custom_call" | custom-call | tf_op jit(solution)/shard_map/pallas_call | solution.py:305
  83.7 0.6 copy.13
  84.3 0.9 %copy.14 = f32[4,192,192]{2,1,0:T(8,128)} copy(f32[4,192,192]{2,1,0:T(8,128)S(1)} %bitcast.2) | data formatting | bytes 1179648
Async XLA Ops:
  0.6 0.7 copy-start.8
  1.3 1.0 %copy-start = (f32[10,96,96]{2,1,0:T(8,128)S(1)}, f32[10,96,96]{2,1,0:T(8,128)}, u32[]{:S(2)}) copy-start(f32[10,96,96]{2,1,0:T(8,128)} %xr_ref.1) | copy-start | bytes 1105924
  2.3 1.0 %copy-start.1 = (f32[10,96,96]{2,1,0:T(8,128)S(1)}, f32[10,96,96]{2,1,0:T(8,128)}, u32[]{:S(2)}) copy-start(f32[10,96,96]{2,1,0:T(8,128)} %xi_ref.1) | copy-start | bytes 1105924
  3.4 0.9 %copy-start.2 = (f32[4,96,96]{2,1,0:T(8,128)S(1)}, f32[4,96,96]{2,1,0:T(8,128)}, u32[]{:S(2)}) copy-start(f32[4,96,96]{2,1,0:T(8,128)} %tr_ref.1) | copy-start | bytes 442372
  4.3 0.9 %copy-start.3 = (f32[4,96,96]{2,1,0:T(8,128)S(1)}, f32[4,96,96]{2,1,0:T(8,128)}, u32[]{:S(2)}) copy-start(f32[4,96,96]{2,1,0:T(8,128)} %ti_ref.1) | copy-start | bytes 442372
  5.2 0.9 %copy-start.4 = (f32[192,128]{1,0:T(8,128)S(1)}, f32[192,128]{1,0:T(8,128)}, u32[]{:S(2)}) copy-start(f32[192,128]{1,0:T(8,128)} %f_ref.1) | copy-start | bytes 294916
  6.1 0.9 %copy-start.5 = (f32[192,128]{1,0:T(8,128)S(1)}, f32[192,128]{1,0:T(8,128)}, u32[]{:S(2)}) copy-start(f32[192,128]{1,0:T(8,128)} %inc_ref.1) | copy-start | bytes 294916
  7.0 0.9 %copy-start.6 = (f32[192,128]{1,0:T(8,128)S(1)}, f32[192,128]{1,0:T(8,128)}, u32[]{:S(2)}) copy-start(f32[192,128]{1,0:T(8,128)} %g_ref.1) | copy-start | bytes 294916
  7.9 0.7 copy-start.7

commit v2 on v1

--- a/solution.py
+++ b/solution.py
@@ -32,15 +32,17 @@
     f_ref, inc_ref, g_ref, tr_ref, ti_ref, xr_ref, xi_ref, nbr_ref, kind_ref,
     adj_ref, sens_ref,
     t_hi, t_lo, w_hi, w_lo, one_ref, two_ref, y_hi, y_lo, fext, pack, coll, part, work,
-    s_all, s_recv, s_mine, s_out, gram, gram_recv,
-    f_send, f_recv, p_send, p_recv, gram_sem, rs_send, rs_recv, ag_sem,
+    s_all, s_twin, s_recv, s_mine, s_out, gram, gram_recv,
+    f_send, f_recv, p_send, p_recv, gram_sem, twin_send, twin_recv, rs_send, rs_recv,
+    ag_send, ag_recv, pass_sem,
 ):
     width, count = f_ref.shape
     half = width // 2
     kinds, slots = tr_ref.shape[0], xr_ref.shape[0]
     rows = count // COLS
     devices = n_gx * n_gy
-    owners = kinds * width // chunk
+    part_rows = kinds * width // 2
+    owners = part_rows // chunk
     gx, gy = lax.axis_index("gx"), lax.axis_index("gy")
     me = gx * n_gy + gy
 
@@ -50,6 +52,26 @@
             body(j, peer, (peer // n_gy, lax.rem(peer, n_gy)))
             return carry
         lax.fori_loop(0, devices - 1, step, 0)
+
+    core, team, mine = lax.rem(gy, 2), devices // 2, me // 2
+    twin = (gx, gy + 1 - 2 * core)
+    half_gy = n_gy // 2
+
+    def each_mate(body):
+        def step(j, carry):
+            mate = lax.rem(mine + 1 + j, team)
+            body(j, mate, (mate // half_gy, lax.rem(mate, half_gy) * 2 + core))
+            return carry
+        lax.fori_loop(0, team - 1, step, 0)
+
+    def if_owner(number, act):
+        if owners == team:
+            act()
+        else:
+            pl.when(number < owners)(act)
+
+    def chunk_of(number):
+        return pl.ds(pl.multiple_of(number * chunk, 8), chunk)
 
     barrier = pltpu.get_barrier_semaphore()
     each_peer(lambda j, peer, place: pl.semaphore_signal(
@@ -175,24 +197,29 @@
                 work[where, :] += part[index, pl.ds(start + REACH * r, REACH), :]
         return work[...]
 
-    def scatter_terms(index, field, exciting):
+    def gradient_terms(index, field, exciting):
         hi, lo = split(field)
-        for k in range(kinds):
-            mask = jnp.where(kind_row == k, 1.0, 0.0).astype(BF16)
-            s_all[index, pl.ds(k * width, width), :] = dot3((hi * mask, lo * mask), exciting)
-
-        def send(j, peer, place):
-            def go():
+        per = kinds // 2
+        for where, base in ((0, 1 - core), (1, core)):
+            for i in range(per):
+                mask = jnp.where(kind_row == base * per + i, 1.0, 0.0).astype(BF16)
+                s_all[index, where, pl.ds(i * width, width), :] = dot3((hi * mask, lo * mask), exciting)
+            if where == 0:
                 pltpu.make_async_remote_copy(
-                    src_ref=s_all.at[index, pl.ds(pl.multiple_of(peer * chunk, 8), chunk)],
-                    dst_ref=s_recv.at[index, devices - 2 - j],
-                    send_sem=rs_send.at[index], recv_sem=rs_recv.at[index],
-                    device_id=place, device_id_type=MESH).start()
-            if owners == devices:
-                go()
-            else:
-                pl.when(peer < owners)(go)
-        each_peer(send)
+                    src_ref=s_all.at[index, 0], dst_ref=s_twin.at[index],
+                    send_sem=twin_send.at[index], recv_sem=twin_recv.at[index],
+                    device_id=twin, device_id_type=MESH).start()
+
+    def send_terms(index):
+        wait_bytes(twin_recv.at[index], s_twin.at[index])
+        s_all[index, 1] += s_twin[index]
+
+        def send(j, mate, place):
+            if_owner(mate, lambda: pltpu.make_async_remote_copy(
+                src_ref=s_all.at[index, 1, chunk_of(mate)], dst_ref=s_recv.at[index, team - 2 - j],
+                send_sem=rs_send.at[index], recv_sem=rs_recv.at[index],
+                device_id=place, device_id_type=MESH).start())
+        each_mate(send)
 
     def wait_bytes(sem, ref):
         pltpu.make_async_copy(ref, ref, sem).wait()
@@ -209,25 +236,30 @@
         pair = (dot(pick, ext[0]).astype(BF16), dot(pick, ext[1]).astype(BF16))
         exciting_t = exciting_t + dot3(pair, (w_hi[s], w_lo[s]), 1)
     exciting = split(exciting_t)
-    scatter_terms(0, g_ref[...], exciting)
+    gradient_terms(0, g_ref[...], exciting)
 
     q0_t = pull(0, first)
+    send_terms(0)
     second = push(1, q0_t)
     q0 = q0_t.T
-    scatter_terms(1, q0, exciting)
+    gradient_terms(1, q0, exciting)
     q1_t = pull(1, second)
 
+    lane = lax.broadcasted_iota(jnp.int32, (1, 128), 1)
+    local = jnp.zeros((1, 128), F32)
     for i, (a, b) in enumerate(
         ((g_t, g_t), (g_t, q0_t), (q0_t, q0_t), (g_t, q1_t), (q0_t, q1_t), (q1_t, q1_t))
     ):
-        gram[i:i + 1, :] = jnp.sum(a * b, axis=0, keepdims=True)
-    gram[6:8, :] = jnp.zeros((2, width), F32)
+        product = jnp.sum(jnp.sum(a * b, axis=0, keepdims=True), axis=1, keepdims=True)
+        local = jnp.where(lane == i, product, local)
+    gram[...] = local
     each_peer(lambda j, peer, place: pltpu.make_async_remote_copy(
         src_ref=gram, dst_ref=gram_recv.at[devices - 2 - j],
         send_sem=gram_sem.at[0], recv_sem=gram_sem.at[1], device_id=place, device_id_type=MESH).start())
+    send_terms(1)
     wait_bytes(gram_sem.at[1], gram_recv)
-    sums = jnp.sum(gram[...] + jnp.sum(gram_recv[...], axis=0), axis=1, keepdims=True)
-    gg, gq, qq, gv, qv, vv = (sums[i:i + 1, :] for i in range(6))
+    sums = local + jnp.sum(gram_recv[...], axis=0)
+    gg, gq, qq, gv, qv, vv = (sums[:, i:i + 1] for i in range(6))
 
     beta = jnp.sqrt(gg)
     c = gq / gg
@@ -254,39 +286,56 @@
     from_g, from_q = w0 / beta + w1 * c / p1, -w1 / p1
     adj_ref[...] = from_g * g_ref[...] + from_q * q0
 
+    def hand_over(number):
+        pltpu.make_async_remote_copy(
+            src_ref=s_out.at[core, chunk_of(number)], dst_ref=s_out.at[core, chunk_of(number)],
+            send_sem=pass_sem.at[0], recv_sem=pass_sem.at[1], device_id=twin, device_id_type=MESH).start()
+
     def reduce_mine():
         total = []
         for index in range(2):
             wait_bytes(rs_recv.at[index], s_recv.at[index])
-            own = s_all[index, pl.ds(pl.multiple_of(me * chunk, 8), chunk), :]
-            total.append(own + jnp.sum(s_recv[index], axis=0))
-        mine = from_g * total[0] + from_q * total[1]
-        s_mine[...] = mine
-        each_peer(lambda j, peer, place: pltpu.make_async_remote_copy(
-            src_ref=s_mine, dst_ref=s_out.at[pl.ds(pl.multiple_of(me * chunk, 8), chunk)],
-            send_sem=ag_sem.at[0], recv_sem=ag_sem.at[1], device_id=place, device_id_type=MESH).start())
-        s_out[pl.ds(pl.multiple_of(me * chunk, 8), chunk), :] = mine
-        if owners > 1:
-            wait_bytes(ag_sem.at[1], s_out.at[pl.ds(0, (owners - 1) * chunk)])
-            for index in range(2):
-                wait_bytes(rs_send.at[index], s_all.at[index, pl.ds(0, (owners - 1) * chunk)])
-        wait_bytes(ag_sem.at[0], s_recv.at[0])
-
-    if owners == devices:
-        reduce_mine()
-    else:
-        pl.when(me < owners)(reduce_mine)
-
-        @pl.when(me >= owners)
-        def _():
-            wait_bytes(ag_sem.at[1], s_out)
-            for index in range(2):
-                wait_bytes(rs_send.at[index], s_all.at[index])
-
-    sens_ref[...] = s_out[...]
+            total.append(s_all[index, 1, chunk_of(mine), :] + jnp.sum(s_recv[index], axis=0))
+        done = from_g * total[0] + from_q * total[1]
+        s_mine[...] = done
+        each_mate(lambda j, mate, place: pltpu.make_async_remote_copy(
+            src_ref=s_mine, dst_ref=s_out.at[core, chunk_of(mine)],
+            send_sem=ag_send.at[0], recv_sem=ag_recv.at[j], device_id=place, device_id_type=MESH).start())
+        s_out[core, chunk_of(mine), :] = done
+        hand_over(mine)
+
+    if_owner(mine, reduce_mine)
+
+    def relay(j, carry):
+        source = lax.rem(mine - 1 - j + team, team)
+
+        def act():
+            wait_bytes(ag_recv.at[j], s_mine)
+            hand_over(source)
+        if_owner(source, act)
+        return carry
+    lax.fori_loop(0, team - 1, relay, 0)
+    wait_bytes(pass_sem.at[1], s_out.at[0])
+
+    for i in range(2):
+        sens_ref[pl.ds(i * part_rows, part_rows), :] = s_out[i]
     for copy in f_copies + first + second:
         copy.wait_send()
     wait_bytes(gram_sem.at[0], gram_recv)
+    wait_bytes(pass_sem.at[0], s_out.at[0])
+    for index in range(2):
+        wait_bytes(twin_send.at[index], s_all.at[index, 0])
+    if owners > 1 or owners < team:
+        def settle(number):
+            if number:
+                for index in range(2):
+                    wait_bytes(rs_send.at[index], s_all.at[index, 0, pl.ds(0, number * chunk)])
+        if owners == team:
+            settle(owners - 1)
+        else:
+            pl.when(mine < owners)(lambda: settle(owners - 1))
+            pl.when(mine >= owners)(lambda: settle(owners))
+    if_owner(mine, lambda: wait_bytes(ag_send.at[0], s_recv.at[0]))
 
 
 def body(n_gx, n_gy, forward_coeff, incident, cost_grad, tmat_real, tmat_imag, translation_real,
@@ -299,7 +348,7 @@
     extent = count + halo
     total = kinds * width
     chunk = 8
-    while total % chunk or total // chunk > devices:
+    while (total // 2) % chunk or total // 2 // chunk > devices // 2:
         chunk += 8
     vmem = [pl.BlockSpec(memory_space=pltpu.VMEM)]
     adjoint, sensitivity = pl.pallas_call(
@@ -324,12 +373,13 @@
             pltpu.VMEM((2, extent, width), F32),
             pltpu.VMEM((2, halo, width), F32),
             pltpu.VMEM((count, width), F32),
-            pltpu.VMEM((2, total, width), F32),
-            pltpu.VMEM((2, devices - 1, chunk, width), F32),
+            pltpu.VMEM((2, 2, total // 2, width), F32),
+            pltpu.VMEM((2, total // 2, width), F32),
+            pltpu.VMEM((2, devices // 2 - 1, chunk, width), F32),
             pltpu.VMEM((chunk, width), F32),
-            pltpu.VMEM((total, width), F32),
-            pltpu.VMEM((8, width), F32),
-            pltpu.VMEM((devices - 1, 8, width), F32),
+            pltpu.VMEM((2, total // 2, width), F32),
+            pltpu.VMEM((1, 128), F32),
+            pltpu.VMEM((devices - 1, 1, 128), F32),
             pltpu.SemaphoreType.DMA((8,)),
             pltpu.SemaphoreType.DMA((8,)),
             pltpu.SemaphoreType.DMA((2, 8)),
@@ -337,6 +387,10 @@
             pltpu.SemaphoreType.DMA((2,)),
             pltpu.SemaphoreType.DMA((2,)),
             pltpu.SemaphoreType.DMA((2,)),
+            pltpu.SemaphoreType.DMA((2,)),
+            pltpu.SemaphoreType.DMA((2,)),
+            pltpu.SemaphoreType.DMA((1,)),
+            pltpu.SemaphoreType.DMA((devices // 2 - 1,)),
             pltpu.SemaphoreType.DMA((2,)),
         ],
         compiler_params=pltpu.CompilerParams(

time: 86.5 us -> 59 us (0.68)
  Pallas kernels: 75.1 us -> 47.8 us
    pallas_call x1, Pallas kernels: 75.1 us -> 47.8 us  [body(): pl.pallas_call(functools.partial(kernel, n_gx, n_gy, chunk), out_shape=(j...]
where the time goes in v2:
time: 59 us; the launch traced here: 57.9 us
  Pallas kernels  47.8 us (81%)
  local copies, waits for them, and re-layouts  9.45 us (16%)
  between operations  0.66 us (1%)
    pallas_call x1, Pallas kernels, body(): pl.pallas_call(functools.partial(kernel, n_gx, n_gy, chunk), out_shape=(j...  47.8 us
    unnamed x20, local copies, waits for them, and re-layouts  9.45 us

profile of v2, /device:TPU:13, one launch (start us, length us, event | category | flops | bytes accessed | tf_op | source)
XLA Modules:
  0.0 57.9 jit_solution(10106077370904668171)
XLA Ops:
  0.6 0.0 copy-start.8
  0.6 0.6 %copy-done.8 = s32[128]{0:T(128)S(1)} copy-done((s32[128]{0:T(128)S(1)}, s32[128]{0:T(128)}, u32[]{:S(2)}) %copy-start.8) | copy-done | bytes 536
  1.3 0.0 copy-start
  1.3 1.0 %copy-done = f32[10,96,96]{2,1,0:T(8,128)S(1)} copy-done((f32[10,96,96]{2,1,0:T(8,128)S(1)}, f32[10,96,96]{2,1,0:T(8,128)}, u32[]{:S(2)}) %copy-start) | copy-done | bytes 368664
  2.3 0.0 copy-start.1
  2.3 1.0 %copy-done.1 = f32[10,96,96]{2,1,0:T(8,128)S(1)} copy-done((f32[10,96,96]{2,1,0:T(8,128)S(1)}, f32[10,96,96]{2,1,0:T(8,128)}, u32[]{:S(2)}) %copy-start.1) | copy-done | bytes 368664
  3.4 0.0 copy-start.2
  3.4 0.9 %copy-done.2 = f32[4,96,96]{2,1,0:T(8,128)S(1)} copy-done((f32[4,96,96]{2,1,0:T(8,128)S(1)}, f32[4,96,96]{2,1,0:T(8,128)}, u32[]{:S(2)}) %copy-start.2) | copy-done | bytes 147480
  4.3 0.0 copy-start.3
  4.3 0.9 %copy-done.3 = f32[4,96,96]{2,1,0:T(8,128)S(1)} copy-done((f32[4,96,96]{2,1,0:T(8,128)S(1)}, f32[4,96,96]{2,1,0:T(8,128)}, u32[]{:S(2)}) %copy-start.3) | copy-done | bytes 147480
  5.2 0.0 copy-start.4
  5.2 0.9 %copy-done.4 = f32[192,128]{1,0:T(8,128)S(1)} copy-done((f32[192,128]{1,0:T(8,128)S(1)}, f32[192,128]{1,0:T(8,128)}, u32[]{:S(2)}) %copy-start.4) | copy-done | bytes 98328
  6.1 0.0 copy-start.5
  6.1 0.9 %copy-done.5 = f32[192,128]{1,0:T(8,128)S(1)} copy-done((f32[192,128]{1,0:T(8,128)S(1)}, f32[192,128]{1,0:T(8,128)}, u32[]{:S(2)}) %copy-start.5) | copy-done | bytes 98328
  7.0 0.0 copy-start.6
  7.0 0.9 %copy-done.6 = f32[192,128]{1,0:T(8,128)S(1)} copy-done((f32[192,128]{1,0:T(8,128)S(1)}, f32[192,128]{1,0:T(8,128)}, u32[]{:S(2)}) %copy-start.6) | copy-done | bytes 98328
  7.9 0.0 copy-start.7
  7.9 0.7 %copy-done.7 = s32[10,128]{1,0:T(8,128)S(1)} copy-done((s32[10,128]{1,0:T(8,128)S(1)}, s32[10,128]{1,0:T(8,128)}, u32[]{:S(2)}) %copy-start.7) | copy-done | bytes 5144
  8.6 47.8 %shard_map.104 = (f32[192,128]{1,0:T(8,128)S(1)}, f32[768,192]{1,0:T(8,128)S(1)}) custom-call(f32[192,128]{1,0:T(8,128)S(1)} %copy-done.4, f32[192,128]{1,0:T(8,128)S(1)} %copy-done.5, f32[192,128]{1,0:T(8,128)S(1)} %copy-done.6, f32[4,96,96]{2,1,0:T(8,128)S(1)} %copy-done.2, f32[4,96,96]{2,1,0:T(8,128)S(1)} %copy-done.3, f32[10,96,96]{2,1,0:T(8,128)S(1)} %copy-done, ...), custom_call_target="tpu_custom_call" | custom-call | tf_op jit(solution)/shard_map/pallas_call | solution.py:354
  56.4 0.6 %copy.13 = f32[192,128]{1,0:T(8,128)} copy(f32[192,128]{1,0:T(8,128)S(1)} %get-tuple-element.8) | data formatting | bytes 196608
  57.0 0.9 %copy.14 = f32[4,192,192]{2,1,0:T(8,128)} copy(f32[4,192,192]{2,1,0:T(8,128)S(1)} %bitcast.2) | data formatting | bytes 1179648
Async XLA Ops:
  0.6 0.7 %copy-start.8 = (s32[128]{0:T(128)S(1)}, s32[128]{0:T(128)}, u32[]{:S(2)}) copy-start(s32[128]{0:T(128)} %param.17) | copy-start | bytes 1540
  1.3 1.0 %copy-start = (f32[10,96,96]{2,1,0:T(8,128)S(1)}, f32[10,96,96]{2,1,0:T(8,128)}, u32[]{:S(2)}) copy-start(f32[10,96,96]{2,1,0:T(8,128)} %xr_ref.1) | copy-start | bytes 1105924
  2.3 1.0 %copy-start.1 = (f32[10,96,96]{2,1,0:T(8,128)S(1)}, f32[10,96,96]{2,1,0:T(8,128)}, u32[]{:S(2)}) copy-start(f32[10,96,96]{2,1,0:T(8,128)} %xi_ref.1) | copy-start | bytes 1105924
  3.4 0.9 %copy-start.2 = (f32[4,96,96]{2,1,0:T(8,128)S(1)}, f32[4,96,96]{2,1,0:T(8,128)}, u32[]{:S(2)}) copy-start(f32[4,96,96]{2,1,0:T(8,128)} %tr_ref.1) | copy-start | bytes 442372
  4.3 0.9 %copy-start.3 = (f32[4,96,96]{2,1,0:T(8,128)S(1)}, f32[4,96,96]{2,1,0:T(8,128)}, u32[]{:S(2)}) copy-start(f32[4,96,96]{2,1,0:T(8,128)} %ti_ref.1) | copy-start | bytes 442372
  5.2 0.9 %copy-start.4 = (f32[192,128]{1,0:T(8,128)S(1)}, f32[192,128]{1,0:T(8,128)}, u32[]{:S(2)}) copy-start(f32[192,128]{1,0:T(8,128)} %f_ref.1) | copy-start | bytes 294916
  6.1 0.9 %copy-start.5 = (f32[192,128]{1,0:T(8,128)S(1)}, f32[192,128]{1,0:T(8,128)}, u32[]{:S(2)}) copy-start(f32[192,128]{1,0:T(8,128)} %inc_ref.1) | copy-start | bytes 294916
  7.0 0.9 %copy-start.6 = (f32[192,128]{1,0:T(8,128)S(1)}, f32[192,128]{1,0:T(8,128)}, u32[]{:S(2)}) copy-start(f32[192,128]{1,0:T(8,128)} %g_ref.1) | copy-start | bytes 294916
  7.9 0.7 %copy-start.7 = (s32[10,128]{1,0:T(8,128)S(1)}, s32[10,128]{1,0:T(8,128)}, u32[]{:S(2)}) copy-start(s32[10,128]{1,0:T(8,128)} %nbr_ref.1) | copy-start | bytes 15364

commit v3 on v2

--- a/solution.py
+++ b/solution.py
@@ -29,13 +29,23 @@
 
 def kernel(
     n_gx, n_gy, chunk,
-    f_ref, inc_ref, g_ref, tr_ref, ti_ref, xr_ref, xi_ref, nbr_ref, kind_ref,
+    f_hbm, inc_hbm, g_hbm, tr_hbm, ti_hbm, xr_hbm, xi_hbm, nbr_hbm, kind_hbm,
     adj_ref, sens_ref,
+    f_ref, inc_ref, g_ref, tr_ref, ti_ref, xr_ref, xi_ref, nbr_ref, kind_ref, load_sem,
     t_hi, t_lo, w_hi, w_lo, one_ref, two_ref, y_hi, y_lo, fext, pack, coll, part, work,
     s_all, s_twin, s_recv, s_mine, s_out, gram, gram_recv,
     f_send, f_recv, p_send, p_recv, gram_sem, twin_send, twin_recv, rs_send, rs_recv,
     ag_send, ag_recv, pass_sem,
 ):
+    loads = [
+        pltpu.make_async_copy(src, dst, load_sem.at[i])
+        for i, (src, dst) in enumerate((
+            (f_hbm, f_ref), (nbr_hbm, nbr_ref), (kind_hbm, kind_ref), (tr_hbm, tr_ref), (ti_hbm, ti_ref),
+            (xr_hbm, xr_ref), (xi_hbm, xi_ref), (g_hbm, g_ref), (inc_hbm, inc_ref)))
+    ]
+    for load in loads:
+        load.start()
+
     width, count = f_ref.shape
     half = width // 2
     kinds, slots = tr_ref.shape[0], xr_ref.shape[0]
@@ -102,6 +112,8 @@
         (blocks[7][0], 0, REACH, 0),
     )
 
+    for load in loads[:3]:
+        load.wait()
     fext[pl.ds(0, count), :] = f_ref[...].T
     pack[...] = jnp.zeros_like(pack)
     for start, row, number, column in pieces:
@@ -145,6 +157,8 @@
                 hi_ref[k, pl.ds(start, half), :] = hi
                 lo_ref[k, pl.ds(start, half), :] = lo
 
+    for load in loads[3:]:
+        load.wait()
     prepare(tr_ref, ti_ref, t_hi, t_lo, kinds)
     prepare(xr_ref, xi_ref, w_hi, w_lo, slots)
 
@@ -350,6 +364,8 @@
     chunk = 8
     while (total // 2) % chunk or total // 2 // chunk > devices // 2:
         chunk += 8
+    operands = (forward_coeff, incident, cost_grad, tmat_real, tmat_imag, translation_real,
+                translation_imaginary, neighbours, particle_type.reshape(1, count))
     vmem = [pl.BlockSpec(memory_space=pltpu.VMEM)]
     adjoint, sensitivity = pl.pallas_call(
         functools.partial(kernel, n_gx, n_gy, chunk),
@@ -357,9 +373,10 @@
             jax.ShapeDtypeStruct((width, count), F32),
             jax.ShapeDtypeStruct((total, width), F32),
         ),
-        in_specs=vmem * 9,
+        in_specs=[pl.BlockSpec(memory_space=pltpu.HBM)] * 9,
         out_specs=(vmem[0], vmem[0]),
-        scratch_shapes=[
+        scratch_shapes=[pltpu.VMEM(x.shape, x.dtype) for x in operands] + [
+            pltpu.SemaphoreType.DMA((len(operands),)),
             pltpu.VMEM((kinds, width, width), BF16),
             pltpu.VMEM((kinds, width, width), BF16),
             pltpu.VMEM((slots, width, width), BF16),
@@ -394,9 +411,8 @@
             pltpu.SemaphoreType.DMA((2,)),
         ],
         compiler_params=pltpu.CompilerParams(
-            collective_id=0, has_side_effects=True, vmem_limit_bytes=48 * 1024 * 1024),
-    )(forward_coeff, incident, cost_grad, tmat_real, tmat_imag, translation_real,
-      translation_imaginary, neighbours, particle_type.reshape(1, count))
+            collective_id=0, has_side_effects=True, vmem_limit_bytes=67043328),
+    )(*operands)
     return adjoint, sensitivity.reshape(kinds, width, width)
 
 

time: 59 us -> 55.9 us (0.947); the launches traced: 57.9 us -> 55.7 us
  local copies, waits for them, and re-layouts: 9.45 us -> 3.6 us
  Pallas kernels: 47.8 us -> 51.4 us
    unnamed x20 -> x2, local copies, waits for them, and re-layouts: 9.45 us -> 3.6 us
    pallas_call x1, Pallas kernels: 47.8 us -> 51.4 us  [body(): pl.pallas_call(functools.partial(kernel, n_gx, n_gy, chunk), out_shape=(j...]
where the time goes in v3:
time: 55.9 us; the launch traced here: 55.7 us
  Pallas kernels  51.4 us (92%)
  local copies, waits for them, and re-layouts  3.6 us (6%)
  between operations  0.64 us (1%)
    pallas_call x1, Pallas kernels, body(): pl.pallas_call(functools.partial(kernel, n_gx, n_gy, chunk), out_shape=(j...  51.4 us
    unnamed x2, local copies, waits for them, and re-layouts  3.6 us

profile of v3, /device:TPU:13, one launch (start us, length us, event | category | flops | bytes accessed | tf_op | source)
XLA Modules:
  0.0 55.7 jit_solution(6190493663556648286)
XLA Ops:
  0.6 51.4 %shard_map.104 = (f32[192,128]{1,0:T(8,128)}, f32[768,192]{1,0:T(8,128)}) custom-call(f32[192,128]{1,0:T(8,128)} %f_hbm.1, f32[192,128]{1,0:T(8,128)} %inc_hbm.1, f32[192,128]{1,0:T(8,128)} %g_hbm.1, f32[4,96,96]{2,1,0:T(8,128)} %tr_hbm.1, f32[4,96,96]{2,1,0:T(8,128)} %ti_hbm.1, f32[10,96,96]{2,1,0:T(8,128)} %xr_hbm.1, f32[10,96,96]{2,1,0:T(8,128)} %xi_hbm.1, ...), custom_call_target="tpu_custom_call" | custom-call | tf_op jit(solution)/shard_map/pallas_call | solution.py:370
  52.1 1.5 %copy.13 = f32[192,128]{1,0:T(8,128)} copy(f32[192,128]{1,0:T(8,128)} %get-tuple-element.8) | data formatting | bytes 196608
  53.6 2.1 %copy.14 = f32[4,192,192]{2,1,0:T(8,128)} copy(f32[4,192,192]{2,1,0:T(8,128)} %bitcast.2) | data formatting | bytes 1179648
